TPU v7x, 32 devices: a whole 2x2x4 slice. The times are simulated.
32 devices in a mesh: fsdp: 8 (over y, x, core), seq: 4 (over z).
Axes of the slice: x: 2, y: 2, z: 4, core: 2. Of those that a mesh axis runs over, the one named last changes fastest.
Arguments:
- tokens: bfloat16 [16, 2048, 768], P('fsdp', 'seq'), may hold values from -6 to 6
- teacher: bfloat16 [16, 2048, 768], P('fsdp', 'seq'), may hold values from -6 to 6
- segment_ids: int32 [16, 2048], P('fsdp', 'seq'), may hold values from 0 to 3, as said below
- latent_flags: int32 [16, 2048], P('fsdp', 'seq'), may hold values from 0 to 1, as said below
- valid_mask: int32 [16, 2048], P('fsdp', 'seq'), may hold values from 0 to 1, as said below
- attngain: bfloat16 [768], P('fsdp'), may hold values from 0.5 to 1.5
- attnshift: bfloat16 [768], P('fsdp'), may hold values from -4 to 4
- qkvweight: bfloat16 [768, 2304], P('fsdp'), may hold values from -0.3125 to 0.3125
- qvbias: bfloat16 [1536], P('fsdp'), may hold values from -4 to 4
- outweight: bfloat16 [768, 768], P('fsdp'), may hold values from -0.875 to 0.875
- outbias: bfloat16 [768], P('fsdp'), may hold values from -4 to 4
- mlpgain: bfloat16 [768], P('fsdp'), may hold values from 0.5 to 1.5
- mlpshift: bfloat16 [768], P('fsdp'), may hold values from -4 to 4
- fcweight: bfloat16 [768, 3072], P('fsdp'), may hold values from -0.21875 to 0.21875
- fcbias: bfloat16 [3072], P('fsdp'), may hold values from -6 to 6
- projweight: bfloat16 [3072, 768], P('fsdp'), may hold values from -0.109375 to 0.109375
- projbias: bfloat16 [768], P('fsdp'), may hold values from -4 to 4
Outputs:
- distill_loss: float32 [], replicated
- layer_out: bfloat16 [16, 2048, 768], P('fsdp', 'seq')
- grad_tokens: bfloat16 [16, 2048, 768], P('fsdp', 'seq')
- grad_attngain: float32 [768], P('fsdp')
- grad_attnshift: float32 [768], P('fsdp')
- grad_qkvweight: float32 [768, 2304], P('fsdp')
- grad_qvbias: float32 [1536], P('fsdp')
- grad_outweight: float32 [768, 768], P('fsdp')
- grad_outbias: float32 [768], P('fsdp')
- grad_mlpgain: float32 [768], P('fsdp')
- grad_mlpshift: float32 [768], P('fsdp')
- grad_fcweight: float32 [768, 3072], P('fsdp')
- grad_fcbias: float32 [3072], P('fsdp')
- grad_projweight: float32 [3072, 768], P('fsdp')
- grad_projbias: float32 [768], P('fsdp')
Inputs may be any that keep to these rules, and one draw needn't show every extreme that they name: `segment_ids`: ids never fall along a sequence, start at 0, and every sequence holds four documents. `latent_flags`: the first token of every sequence is not latent. `valid_mask`: the first token of every sequence is valid.
All inputs are finite; a program needn't handle non-finite values.
Results may differ from a plain program's by a relative error of at most 0.012.
The roundings to bfloat16 on the way count: a program that leaves them out, or rounds other values in their place, can miss the bound.
Values may be sent and summed in bfloat16 or wider, within the bound.
No kernel may reach another device: no remote copies, remote signals or barrier semaphores. Data moves between devices by JAX's collectives and lax.ppermute only.
A program may use at most 256 MiB of HBM per device.

v0:
```python
import math
import jax
import jax.numpy as jnp
from jax import lax
from jax.sharding import PartitionSpec as P

H = 12
HD = 64
EPSILON = 1e-05


def for_sending(x):

    def short(part):
        return part.astype(jnp.bfloat16) if part.dtype == jnp.float32 else part

    return jax.tree.map(short, x)


def layer_norm(values, gain, shift):
    center = values - jnp.mean(values, -1, keepdims=True)
    spread = jnp.mean(center * center, -1, keepdims=True)
    return center * lax.rsqrt(spread + EPSILON) * gain + shift


def gelu_tanh(values):
    inner = 0.7978845608028654 * (values + 0.044715 * values * values * values)
    return 0.5 * values * (1.0 + jnp.tanh(inner))


def split_heads(joint_item):
    length = joint_item.shape[0]
    heads_local = joint_item.shape[-1] // HD
    query = joint_item[:, 0, 0].reshape(length, heads_local, HD)
    keys = joint_item[:, 1, 0].reshape(length, heads_local, HD)
    values = joint_item[:, 2, 0].reshape(length, heads_local, HD)
    return (query, keys, values)


def block_scores(query_block, keys, segments, start):
    block = query_block.shape[0]
    length = keys.shape[0]
    scale = 1.0 / math.sqrt(HD)
    scores = (
        jnp.einsum("qhd,khd->hqk", query_block, keys, preferred_element_type=jnp.float32) * scale
    )
    place = jnp.arange(length, dtype=jnp.int32)
    rows_here = place[start : start + block]
    allowed = (place[None, :] <= rows_here[:, None]) & (
        segments[start : start + block, None] == segments[None, :]
    )
    return jnp.where(allowed[None], scores, -1e30)


def attend_sequence(item):
    joint_item, segments = item
    query, keys, values = split_heads(joint_item)
    length = query.shape[0]
    block = min(512, length)
    mixed_blocks = []
    total_blocks = []
    for start in range(0, length, block):
        masked = block_scores(query[start : start + block], keys, segments, start)
        highest = jnp.max(masked, -1, keepdims=True)
        powers = jnp.exp(masked - highest)
        total = jnp.sum(powers, -1, keepdims=True)
        probs = powers / total
        mixed = jnp.einsum(
            "hqk,khd->qhd", probs.astype(jnp.bfloat16), values, preferred_element_type=jnp.float32
        )
        mixed_blocks.append(mixed.reshape(block, -1).astype(jnp.bfloat16))
        total_blocks.append((highest + jnp.log(total))[:, :, 0])
    return (jnp.concatenate(mixed_blocks, 0), jnp.concatenate(total_blocks, 1))


def attend_items(pieces):
    joint_piece, segment_piece = pieces
    segments = segment_piece[:, :, 0, 0, 0]
    mixed, log_total = lax.map(attend_sequence, (joint_piece, segments))
    return (mixed, log_total, joint_piece, segments)


def back_sequence(item):
    joint_item, segments, log_total, grad_mixed = item
    query, keys, values = split_heads(joint_item)
    length, heads_local, _ = query.shape
    grad_out = grad_mixed[:, 0].reshape(length, heads_local, HD)
    block = min(512, length)
    scale = 1.0 / math.sqrt(HD)
    grad_keys = jnp.zeros((length, heads_local, HD), jnp.float32)
    grad_values = jnp.zeros((length, heads_local, HD), jnp.float32)
    query_grads = []
    for start in range(0, length, block):
        query_block = query[start : start + block]
        grad_block = grad_out[start : start + block]
        masked = block_scores(query_block, keys, segments, start)
        probs = jnp.exp(masked - log_total[:, start : start + block, None])
        probs_low = probs.astype(jnp.bfloat16)
        grad_values = grad_values + jnp.einsum(
            "hqk,qhd->khd", probs_low, grad_block, preferred_element_type=jnp.float32
        )
        grad_probs = jnp.einsum(
            "qhd,khd->hqk", grad_block, values, preferred_element_type=jnp.float32
        )
        center = jnp.sum(probs * grad_probs, -1, keepdims=True)
        grad_scores = (probs * (grad_probs - center)).astype(jnp.bfloat16)
        query_grads.append(
            jnp.einsum("hqk,khd->qhd", grad_scores, keys, preferred_element_type=jnp.float32)
            * scale
        )
        grad_keys = (
            grad_keys
            + jnp.einsum(
                "hqk,qhd->khd", grad_scores, query_block, preferred_element_type=jnp.float32
            )
            * scale
        )
    grad_query = jnp.concatenate(query_grads, 0)
    stacked = jnp.stack([grad_query, grad_keys, grad_values], 1).astype(jnp.bfloat16)
    return stacked.reshape(length, 3, 1, heads_local * HD)


def local(
    tokens,
    teacher,
    segment_ids,
    latent_flags,
    valid_mask,
    attngain,
    attnshift,
    qkvweight,
    qvbias,
    outweight,
    outbias,
    mlpgain,
    mlpshift,
    fcweight,
    fcbias,
    projweight,
    projbias,
):
    seqs_local, block_len, width = tokens.shape
    groups = lax.axis_size("seq")
    heads_local = H // groups
    rows = seqs_local * block_len
    weight = (valid_mask * (1 - latent_flags)).astype(jnp.float32).reshape(rows)
    local_count = jnp.sum(weight)
    gathered = (
        lax.all_gather(attngain, "fsdp", axis=0, tiled=True),
        lax.all_gather(attnshift, "fsdp", axis=0, tiled=True),
        lax.all_gather(qkvweight, "fsdp", axis=0, tiled=True),
        lax.all_gather(qvbias, "fsdp", axis=0, tiled=True),
        lax.all_gather(outweight, "fsdp", axis=0, tiled=True),
        lax.all_gather(outbias, "fsdp", axis=0, tiled=True),
        lax.all_gather(mlpgain, "fsdp", axis=0, tiled=True),
        lax.all_gather(mlpshift, "fsdp", axis=0, tiled=True),
        lax.all_gather(fcweight, "fsdp", axis=0, tiled=True),
        lax.all_gather(fcbias, "fsdp", axis=0, tiled=True),
        lax.all_gather(projweight, "fsdp", axis=0, tiled=True),
        lax.all_gather(projbias, "fsdp", axis=0, tiled=True),
    )
    first_gain = gathered[0].astype(jnp.float32)
    first_shift = gathered[1].astype(jnp.float32)
    joint_weight = gathered[2]
    joint_bias = gathered[3].astype(jnp.float32)
    merge_weight = gathered[4]
    merge_bias = gathered[5].astype(jnp.float32)
    second_gain = gathered[6].astype(jnp.float32)
    second_shift = gathered[7].astype(jnp.float32)
    up_weight = gathered[8]
    up_bias = gathered[9].astype(jnp.float32)
    down_weight = gathered[10]
    down_bias = gathered[11].astype(jnp.float32)
    inputs = tokens.astype(jnp.float32).reshape(rows, width)
    normed, first_back = jax.vjp(layer_norm, inputs, first_gain, first_shift)
    normed_low = normed.astype(jnp.bfloat16)
    bias_full = jnp.concatenate(
        [joint_bias[:width], jnp.zeros((width,), jnp.float32), joint_bias[width:]]
    )
    joint = jnp.dot(normed_low, joint_weight, preferred_element_type=jnp.float32) + bias_full
    joint_low = joint.astype(jnp.bfloat16).reshape(
        seqs_local, block_len, 3, groups, heads_local * HD
    )
    segment_low = jnp.broadcast_to(
        segment_ids.astype(jnp.bfloat16)[:, :, None, None, None],
        (seqs_local, block_len, 1, groups, 1),
    )
    mixed, log_total, kept_joint, kept_segment = attend_items(
        (
            lax.all_to_all(joint_low, "seq", split_axis=3, concat_axis=1, tiled=True),
            lax.all_to_all(segment_low, "seq", split_axis=3, concat_axis=1, tiled=True),
        )
    )
    length = mixed.shape[1]
    mixed_back = lax.all_to_all(
        for_sending(mixed.reshape(seqs_local, length, 1, heads_local * HD)),
        "seq",
        split_axis=1,
        concat_axis=2,
        tiled=True,
    )
    attended = mixed_back.reshape(rows, width)
    branch = jnp.dot(attended, merge_weight, preferred_element_type=jnp.float32) + merge_bias
    resid = inputs + branch
    normed_two, second_back = jax.vjp(layer_norm, resid, second_gain, second_shift)
    normed_two_low = normed_two.astype(jnp.bfloat16)
    hidden = jnp.dot(normed_two_low, up_weight, preferred_element_type=jnp.float32) + up_bias
    active, gelu_back = jax.vjp(gelu_tanh, hidden)
    active_low = active.astype(jnp.bfloat16)
    result = (
        resid + jnp.dot(active_low, down_weight, preferred_element_type=jnp.float32) + down_bias
    )
    layer_out = result.astype(jnp.bfloat16).reshape(tokens.shape)
    error = result - teacher.astype(jnp.float32).reshape(rows, width)
    local_sum = jnp.sum(weight * jnp.sum(error * error, -1))
    total_sum, total_count = lax.psum((local_sum, local_count), ("fsdp", "seq"))
    distill_loss = total_sum / (width * total_count)
    token_total = rows * lax.axis_size("fsdp") * groups
    factor = token_total / total_count
    grad_result = error * (weight * factor)[:, None]
    back_params = (
        lax.all_gather(attngain, "fsdp", axis=0, tiled=True),
        lax.all_gather(attnshift, "fsdp", axis=0, tiled=True),
        lax.all_gather(qkvweight, "fsdp", axis=0, tiled=True),
        lax.all_gather(qvbias, "fsdp", axis=0, tiled=True),
        lax.all_gather(outweight, "fsdp", axis=0, tiled=True),
        lax.all_gather(outbias, "fsdp", axis=0, tiled=True),
        lax.all_gather(mlpgain, "fsdp", axis=0, tiled=True),
        lax.all_gather(mlpshift, "fsdp", axis=0, tiled=True),
        lax.all_gather(fcweight, "fsdp", axis=0, tiled=True),
        lax.all_gather(fcbias, "fsdp", axis=0, tiled=True),
        lax.all_gather(projweight, "fsdp", axis=0, tiled=True),
        lax.all_gather(projbias, "fsdp", axis=0, tiled=True),
    )
    joint_weight = back_params[2]
    merge_weight = back_params[4]
    up_weight = back_params[8]
    down_weight = back_params[10]
    grad_mlp = grad_result.astype(jnp.bfloat16)
    grad_downbias = jnp.sum(grad_mlp, 0, dtype=jnp.float32)
    grad_downweight = jnp.einsum(
        "rf,rd->fd", active_low, grad_mlp, preferred_element_type=jnp.float32
    )
    grad_active = jnp.einsum("rd,fd->rf", grad_mlp, down_weight, preferred_element_type=jnp.float32)
    grad_hidden = gelu_back(grad_active)[0].astype(jnp.bfloat16)
    grad_upbias = jnp.sum(grad_hidden, 0, dtype=jnp.float32)
    grad_upweight = jnp.einsum(
        "rd,rf->df", normed_two_low, grad_hidden, preferred_element_type=jnp.float32
    )
    grad_normed_two = jnp.einsum(
        "rf,df->rd", grad_hidden, up_weight, preferred_element_type=jnp.float32
    )
    resid_part, grad_secondgain, grad_secondshift = second_back(grad_normed_two)
    grad_resid = grad_result + resid_part
    grad_branch = grad_resid.astype(jnp.bfloat16)
    grad_mergebias = jnp.sum(grad_branch, 0, dtype=jnp.float32)
    grad_mergeweight = jnp.einsum(
        "rd,re->de", attended, grad_branch, preferred_element_type=jnp.float32
    )
    grad_attended = jnp.einsum(
        "re,de->rd", grad_branch, merge_weight, preferred_element_type=jnp.float32
    ).astype(jnp.bfloat16)
    grad_heads = lax.all_to_all(
        grad_attended.reshape(seqs_local, block_len, groups, heads_local * HD),
        "seq",
        split_axis=2,
        concat_axis=1,
        tiled=True,
    )
    grad_joint_heads = lax.map(back_sequence, (kept_joint, kept_segment, log_total, grad_heads))
    grad_joint = lax.all_to_all(
        grad_joint_heads, "seq", split_axis=1, concat_axis=3, tiled=True
    ).reshape(rows, 3 * width)
    grad_jointweight = jnp.einsum(
        "rd,re->de", normed_low, grad_joint, preferred_element_type=jnp.float32
    )
    column_sums = jnp.sum(grad_joint, 0, dtype=jnp.float32)
    grad_jointbias = jnp.concatenate([column_sums[:width], column_sums[2 * width :]])
    grad_normed = jnp.einsum(
        "re,de->rd", grad_joint, joint_weight, preferred_element_type=jnp.float32
    )
    input_part, grad_firstgain, grad_firstshift = first_back(grad_normed)
    grad_tokens = (grad_resid + input_part).astype(jnp.bfloat16).reshape(tokens.shape)
    shards = (
        lax.psum_scatter(grad_firstgain, "fsdp", scatter_dimension=0, tiled=True),
        lax.psum_scatter(grad_firstshift, "fsdp", scatter_dimension=0, tiled=True),
        lax.psum_scatter(grad_jointweight, "fsdp", scatter_dimension=0, tiled=True),
        lax.psum_scatter(grad_jointbias, "fsdp", scatter_dimension=0, tiled=True),
        lax.psum_scatter(grad_mergeweight, "fsdp", scatter_dimension=0, tiled=True),
        lax.psum_scatter(grad_mergebias, "fsdp", scatter_dimension=0, tiled=True),
        lax.psum_scatter(grad_secondgain, "fsdp", scatter_dimension=0, tiled=True),
        lax.psum_scatter(grad_secondshift, "fsdp", scatter_dimension=0, tiled=True),
        lax.psum_scatter(grad_upweight, "fsdp", scatter_dimension=0, tiled=True),
        lax.psum_scatter(grad_upbias, "fsdp", scatter_dimension=0, tiled=True),
        lax.psum_scatter(grad_downweight, "fsdp", scatter_dimension=0, tiled=True),
        lax.psum_scatter(grad_downbias, "fsdp", scatter_dimension=0, tiled=True),
    )
    summed = (
        lax.psum(shards[0].astype(jnp.bfloat16), "seq").astype(jnp.float32),
        lax.psum(shards[1].astype(jnp.bfloat16), "seq").astype(jnp.float32),
        lax.psum(shards[2].astype(jnp.bfloat16), "seq").astype(jnp.float32),
        lax.psum(shards[3].astype(jnp.bfloat16), "seq").astype(jnp.float32),
        lax.psum(shards[4].astype(jnp.bfloat16), "seq").astype(jnp.float32),
        lax.psum(shards[5].astype(jnp.bfloat16), "seq").astype(jnp.float32),
        lax.psum(shards[6].astype(jnp.bfloat16), "seq").astype(jnp.float32),
        lax.psum(shards[7].astype(jnp.bfloat16), "seq").astype(jnp.float32),
        lax.psum(shards[8].astype(jnp.bfloat16), "seq").astype(jnp.float32),
        lax.psum(shards[9].astype(jnp.bfloat16), "seq").astype(jnp.float32),
        lax.psum(shards[10].astype(jnp.bfloat16), "seq").astype(jnp.float32),
        lax.psum(shards[11].astype(jnp.bfloat16), "seq").astype(jnp.float32),
    )
    return (
        distill_loss,
        layer_out,
        grad_tokens,
        summed[0],
        summed[1],
        summed[2],
        summed[3],
        summed[4],
        summed[5],
        summed[6],
        summed[7],
        summed[8],
        summed[9],
        summed[10],
        summed[11],
    )


def solution(mesh):
    placed = (
        P("fsdp", "seq", None),
        P("fsdp", "seq", None),
        P("fsdp", "seq"),
        P("fsdp", "seq"),
        P("fsdp", "seq"),
        P("fsdp"),
        P("fsdp"),
        P("fsdp", None),
        P("fsdp"),
        P("fsdp", None),
        P("fsdp"),
        P("fsdp"),
        P("fsdp"),
        P("fsdp", None),
        P("fsdp"),
        P("fsdp", None),
        P("fsdp"),
    )
    return jax.shard_map(
        local,
        mesh=mesh,
        in_specs=placed,
        out_specs=(
            P(),
            P("fsdp", "seq", None),
            P("fsdp", "seq", None),
            P("fsdp"),
            P("fsdp"),
            P("fsdp", None),
            P("fsdp"),
            P("fsdp", None),
            P("fsdp"),
            P("fsdp"),
            P("fsdp"),
            P("fsdp", None),
            P("fsdp"),
            P("fsdp", None),
            P("fsdp"),
        ),
        check_vma=False,
    )
```

profile of v0, /device:TPU:0, one launch (start us, length us, event | category | flops | bytes accessed | tf_op | source)
XLA Modules:
  0.0 1246.0 jit_solution(2136501249223661194)
XLA Ops:
  19.6 26.6 %all-reduce.17 = (bf16[768]{0:T(1024)(128)(2,1)S(1)}, bf16[768]{0:T(1024)(128)(2,1)S(1)}, bf16[1536]{0:T(1024)(128)(2,1)S(1)}, bf16[768]{0:T(1024)(128)(2,1)}, b...) all-reduce(bf16[768]{0:T(1024)(128)(2,1)S(1)} %dynamic-update-slice, ...), channel_id=1, replica_groups=mesh['fsdp'=8,'seq'=4] {'fsdp'}, use_global_device_ids=true, to_apply=%add.1 | all-reduce | flops 6144 | bytes 24576
  50.1 7.5 add_convert_fusion
  57.7 12.8 %reshape.747 = bf16[2,512,3,4,192]{4,3,2,1,0:T(4,128)(2,1)} reshape(bf16[1024,2304]{1,0:T(8,128)(2,1)} %add_convert_fusion) | data formatting | bytes 9437184 | tf_op jit(solution)/shard_map/reshape | solution.py:181
  70.5 17.3 %copy.86 = bf16[2,512,3,4,192]{1,0,4,2,3:T(2,128)(2,1)} copy(bf16[2,512,3,4,192]{4,3,2,1,0:T(4,128)(2,1)} %reshape.747) | data formatting | bytes 9437184 | tf_op jit(solution)/shard_map/reshape | solution.py:181
  87.8 5.1 all-to-all-start
  92.9 101.8 %all-to-all-done = bf16[2,512,3,4,192]{1,0,4,2,3:T(2,128)(2,1)} async-done(((bf16[2,512,3,4,192]{1,0,4,2,3:T(2,128)(2,1)}), bf16[2,512,3,4,192]{1,0,4,2,3:T(2,128)(2,1)}, u32[]{:S(2)}, u32[]{:S(2)}) %all-to-all-start) | async-done | bytes 4718624 | tf_op jit(solution)/shard_map/all_to_all | solution.py:190
  199.1 8.2 copy.87
  207.3 8.8 all_to_all.62
  216.1 113.0 %while.22 = (s32[]{:T(128)}, bf16[2,2048,192]{1,2,0:T(8,128)(2,1)}, f32[2,3,2048]{2,1,0:T(4,128)S(1)}, bf16[2,2048,3,1,192]{1,4,2,3,0:T(8,128)(2,1)}, bf16[2,204...) while((s32[]{:T(128)}, bf16[2,2048,192]{1,2,0:T(8,128)(2,1)}, ...), condition=%wide.region_11.12_spmd, body=%wide.region_2.11_spmd.sunk | while | flops 3393599488 | bytes 199532768 | solution.py:79
  243.2 6.9 fusion.302
  263.7 6.9 fusion.307
  291.9 6.9 fusion.302
  312.3 6.9 fusion.307
  329.2 6.1 copy.89
  335.3 5.2 all-to-all-start.2
  340.6 8.9 all-gather
  349.5 38.3 %all-to-all-done.2 = bf16[2,2048,1,192]{3,0,2,1:T(2,128)(2,1)} async-done(((bf16[2,2048,1,192]{3,0,2,1:T(2,128)(2,1)}), bf16[2,2048,1,192]{3,0,2,1:T(2,128)(2,1)}, u32[]{:S(2)}, u32[]{:S(2)}) %all-to-all-start.2) | async-done | bytes 1572896 | tf_op jit(solution)/shard_map/all_to_all | solution.py:195
  387.8 9.3 copy.90
  404.2 11.2 fusion.113
  415.5 13.7 %multiply_reduce_fusion.6 = (f32[1024]{0:T(1024)S(1)}, f32[1024,768]{1,0:T(8,128)}) fusion(bf16[2,512,768]{2,1,0:T(8,128)(2,1)} %param.22, f32[768]{0:T(1024)S(1)} %convert_element_type.248, f32[1024,768]{1,0:T(8,128)S(1)} %copy-done.15, bf16[3072,768]{1,0:T(8,128)(2,1)} %all-gather.12.cloned.1.call-done, f32[1024,3072]{1,0:T(8,128)} %fusion.113, ...), kind=kOutput, calls=%fused_computation.184 | convolution fusion | flops 4868013056 | bytes 25185280 | tf_op jit(solution)/shard_map/dot_general | solution.py:211
  429.8 39.5 %all-reduce.15 = (f32[]{:T(128)}, f32[]{:T(128)}) all-reduce(f32[]{:T(128)} %get-tuple-element.149, f32[]{:T(128)} %get-tuple-element.148), channel_id=1, replica_groups=mesh['fsdp'=8,'seq'=4] {'fsdp','seq'}, use_global_device_ids=true, to_apply=%region_16.17 | all-reduce | flops 2 | bytes 16 | tf_op jit(solution)/shard_map/psum | solution.py:216
  473.6 18.5 %convert_reduce_fusion = (f32[3072]{0:T(1024)}, bf16[1024,3072]{1,0:T(8,128)(2,1)S(1)}) fusion(f32[1024,3072]{1,0:T(8,128)} %fusion.113, f32[3072]{0:T(1024)S(1)} %bitcast.448, bf16[1024,768]{1,0:T(8,128)(2,1)S(1)} %get-tuple-element.202, bf16[3072,768]{1,0:T(8,128)(2,1)} %all-gather.12.cloned.1.call-done), kind=kOutput, calls=%fused_computation.151 | convolution fusion | flops 4916769792 | bytes 25190400 | tf_op jit(solution)/shard_map/rd,fd->rf/dot_general | solution.py:244
  492.1 6.1 multiply_reduce_fusion.4
  507.8 10.7 fusion.112
  532.8 13.0 %fusion.114 = f32[3072,768]{1,0:T(8,128)} fusion(bf16[1024,768]{1,0:T(8,128)(2,1)S(1)} %copy-done.36, f32[1024,3072]{1,0:T(8,128)} %fusion.113, f32[3072]{0:T(1024)S(1)} %bitcast.449), kind=kOutput, calls=%fused_computation.222 | convolution fusion | flops 4863295488 | bytes 23605248 | tf_op jit(solution)/shard_map/rf,rd->fd/dot_general | solution.py:241
  545.8 23.3 %all-to-all-done.3 = bf16[2,512,4,192]{1,0,3,2:T(2,128)(2,1)S(1)} async-done(((bf16[2,512,4,192]{1,0,3,2:T(2,128)(2,1)}), bf16[2,512,4,192]{1,0,3,2:T(2,128)(2,1)S(1)}, u32[]{:S(2)}, u32[]{:S(2)}) %all-to-all-start.3) | async-done | bytes 1572896 | tf_op jit(solution)/shard_map/all_to_all | solution.py:263
  571.6 315.2 %while.23 = (s32[]{:T(128)}, bf16[2,2048,3,1,192]{1,4,3,2,0:T(8,128)(2,1)}, bf16[2,2048,3,1,192]{1,4,2,3,0:T(8,128)(2,1)}, bf16[2,2048]{1,0:T(2,128)(2,1)S(1)}, ...) while((s32[]{:T(128)}, ...), condition=%wide.region_26.27_spmd, body=%wide.region_21.26_spmd.sunk | while | flops 8274178048 | bytes 657154752 | solution.py:270
  586.8 7.6 multiply_reduce_fusion.13
  599.9 8.2 multiply_reduce_fusion.16
  608.1 6.3 fusion.360
  614.4 8.4 fusion.361
  622.7 10.4 multiply_reduce_fusion.14
  633.1 26.1 %multiply_convert_fusion.8 = (bf16[3,512,2048]{2,1,0:T(8,128)(2,1)}, bf16[3,512,2048]{2,1,0:T(8,128)(2,1)}) fusion(f32[3,512,2048]{2,1,0:T(8,128)} %get-tuple-element.454, f32[3,512,2048]{2,1,0:T(8,128)} %copy-done, f32[3,512]{1,0:T(4,128)S(1)} %get-tuple-element.455, f32[3,512]{1,0:T(4,128)S(1)} %get-tuple-element.443, ...), kind=kLoop, calls=%fused_computation.68.clone.1 | loop fusion | flops 37748736 | bytes 65036288 | tf_op jit(solution)/shard_map/while/body/eval_jaxpr/convert_element_type | solution.py:106
  659.2 6.5 fusion.369
  671.3 6.6 fusion.362
  677.9 8.0 fusion.363
  685.9 10.8 multiply_reduce_fusion.15
  696.7 18.2 %multiply_convert_fusion.9 = (bf16[3,512,2048]{2,1,0:T(8,128)(2,1)}, bf16[3,512,2048]{2,1,0:T(8,128)(2,1)}) fusion(f32[3,512,2048]{2,1,0:T(8,128)} %get-tuple-element.460, f32[3,512,2048]{2,1,0:T(8,128)} %fusion.362, f32[3,512]{1,0:T(4,128)} %get-tuple-element.461, f32[3,512]{1,0:T(4,128)S(1)} %get-tuple-element.451, ...), kind=kLoop, calls=%fused_computation.62.clone.1 | loop fusion | flops 37748736 | bytes 65036288 | tf_op jit(solution)/shard_map/while/body/eval_jaxpr/convert_element_type | solution.py:106
  715.0 4.2 convolution_add_fusion.6
  743.2 7.6 multiply_reduce_fusion.13
  756.4 8.1 multiply_reduce_fusion.16
  764.5 6.3 fusion.360
  770.8 7.8 fusion.361
  778.6 10.5 multiply_reduce_fusion.14
  789.1 22.8 %multiply_convert_fusion.8 = (bf16[3,512,2048]{2,1,0:T(8,128)(2,1)}, bf16[3,512,2048]{2,1,0:T(8,128)(2,1)}) fusion(f32[3,512,2048]{2,1,0:T(8,128)} %get-tuple-element.454, f32[3,512,2048]{2,1,0:T(8,128)} %copy-done, f32[3,512]{1,0:T(4,128)S(1)} %get-tuple-element.455, f32[3,512]{1,0:T(4,128)S(1)} %get-tuple-element.443, ...), kind=kLoop, calls=%fused_computation.68.clone.1 | loop fusion | flops 37748736 | bytes 65036288 | tf_op jit(solution)/shard_map/while/body/eval_jaxpr/convert_element_type | solution.py:106
  811.9 5.7 fusion.369
  823.1 6.3 fusion.362
  829.5 7.7 fusion.363
  837.1 10.7 multiply_reduce_fusion.15
  847.8 18.1 %multiply_convert_fusion.9 = (bf16[3,512,2048]{2,1,0:T(8,128)(2,1)}, bf16[3,512,2048]{2,1,0:T(8,128)(2,1)}) fusion(f32[3,512,2048]{2,1,0:T(8,128)} %get-tuple-element.460, f32[3,512,2048]{2,1,0:T(8,128)} %fusion.362, f32[3,512]{1,0:T(4,128)} %get-tuple-element.461, f32[3,512]{1,0:T(4,128)S(1)} %get-tuple-element.451, ...), kind=kLoop, calls=%fused_computation.62.clone.1 | loop fusion | flops 37748736 | bytes 65036288 | tf_op jit(solution)/shard_map/while/body/eval_jaxpr/convert_element_type | solution.py:106
  865.9 4.2 convolution_add_fusion.6
  886.8 16.2 %copy.95 = bf16[2,2048,3,1,192]{4,0,3,2,1:T(2,128)(2,1)} copy(bf16[2,2048,3,1,192]{1,4,3,2,0:T(8,128)(2,1)} %get-tuple-element.77) | data formatting | bytes 9437184 | tf_op jit(solution)/shard_map/while | solution.py:270
  903.0 5.4 all-to-all-start.4
  909.1 137.3 %all-to-all-done.4 = bf16[2,2048,3,1,192]{4,0,3,2,1:T(2,128)(2,1)} async-done(((bf16[2,2048,3,1,192]{4,0,3,2,1:T(2,128)(2,1)}), bf16[2,2048,3,1,192]{4,0,3,2,1:T(2,128)(2,1)}, u32[]{:S(2)}, u32[]{:S(2)}) %all-to-all-start.4) | async-done | bytes 4718624 | tf_op jit(solution)/shard_map/all_to_all | solution.py:271
  1046.4 16.9 %copy.102 = bf16[2,4,512,3,1,192]{2,1,5,3,0,4:T(4,128)(2,1)} copy(bf16[2,4,512,3,1,192]{5,0,3,2,1,4:T(2,128)(2,1)} %bitcast.59) | data formatting | bytes 9437184 | tf_op jit(solution)/shard_map/all_to_all | solution.py:271
  1063.3 9.3 copy.97
  1078.6 6.0 fusion.133
  1089.8 10.6 fusion.117
  1104.7 44.6 %reduce-scatter.5.cloned.1.call-done = f32[96,2304]{1,0:T(8,128)} async-done(((f32[768,2304]{1,0:T(8,128)}), f32[96,2304]{1,0:T(8,128)}) %reduce-scatter.5.cloned.1.call-update) | async-done | bytes 884752 | tf_op jit(solution)/shard_map/reduce_scatter | solution.py:287
  1151.4 4.3 convert_reduce_fusion.1
  1159.2 25.1 %all-reduce.16 = (bf16[768]{0:T(1024)(128)(2,1)S(1)}, bf16[768]{0:T(1024)(128)(2,1)S(1)}, bf16[1536]{0:T(1024)(128)(2,1)S(1)}, bf16[768]{0:T(1024)(128)(2,1)S(1)...) all-reduce(f32[768]{0:T(1024)S(1)} %get-tuple-element.143, ...), channel_id=2, replica_groups=mesh['fsdp'=8,'seq'=4] {'fsdp'}, use_global_device_ids=true, to_apply=%region_30.31.clone | all-reduce | flops 9216 | bytes 55296
  1184.9 11.8 all-reduce.18
  1201.0 4.3 add_convert_fusion.1
  1205.3 24.9 %all-reduce.22.cloned.1.call-done = (bf16[96,2304]{1,0:T(8,128)(2,1)}, bf16[96,768]{1,0:T(8,128)(2,1)}, bf16[96,3072]{1,0:T(8,128)(2,1)}, bf16[384,768]{1,0:T(8,128)(2,1)}) async-done(((bf16[96,2304]{1,0:T(8,128)(2,1)}, bf16[96,768]{1,0:T(8,128)(2,1)}, bf16[96,3072]{1,0:T(8,128)(2,1)}, bf16[384,768]{1,0:T(8,128)(2,1)}), (bf16[96,2304]{1,0:T(8,128)(2,1)}, bf16[96,768]{1,0:T(8,128)(2,1)}, ...) | async-done | bytes 1769488 | tf_op jit(solution)/shard_map/psum | solution.py:301
  (429 shorter events, 226.6 us)
Async XLA Ops:
  7.2 42.3 %copy-start.5 = (bf16[2,512,768]{2,1,0:T(8,128)(2,1)S(1)}, bf16[2,512,768]{2,1,0:T(8,128)(2,1)}, u32[]{:S(2)}) copy-start(bf16[2,512,768]{2,1,0:T(8,128)(2,1)} %param.21) | copy-start | bytes 4718596
  7.2 42.9 %all-gather.6.cloned.1.call-start = ((), (), s32[]{:S(2)}) async-start(), calls=%async_computation.9 | async-start | bytes 3981312 | tf_op jit(solution)/shard_map/all_gather | solution.py:151
  7.9 390.7 %all-gather.8.cloned.1.call-start = ((), (), s32[]{:S(2)}) async-start(), calls=%async_computation.10 | async-start | bytes 1327104 | tf_op jit(solution)/shard_map/all_gather | solution.py:153
  8.7 395.6 %all-gather.10.cloned.1.call-start = ((), (), s32[]{:S(2)}) async-start(), calls=%async_computation.11 | async-start | bytes 5308416 | tf_op jit(solution)/shard_map/all_gather | solution.py:157
  87.8 5.1 copy-start.57
  87.8 106.9 %all-to-all-start = ((bf16[2,512,3,4,192]{1,0,4,2,3:T(2,128)(2,1)}), bf16[2,512,3,4,192]{1,0,4,2,3:T(2,128)(2,1)}, u32[]{:S(2)}, u32[]{:S(2)}) async-start(bf16[2,512,3,4,192]{1,0,4,2,3:T(2,128)(2,1)} %copy.86), calls=%async_computation | async-start | bytes 9437184 | tf_op jit(solution)/shard_map/all_to_all | solution.py:190
  195.3 20.8 %all-to-all-start.1 = ((bf16[2,512,1,4,1]{1,0,4,2,3:T(2,128)(2,1)}), bf16[2,512,1,4,1]{1,0,4,2,3:T(2,128)(2,1)S(1)}, u32[]{:S(2)}, u32[]{:S(2)}) async-start(bf16[2,512,1,4,1]{1,0,4,2,3:T(2,128)(2,1)} %broadcast_in_dim.114), calls=%async_computation.1 | async-start | bytes 16384 | tf_op jit(solution)/shard_map/all_to_all | solution.py:191
  198.5 216.9 %all-gather.12.cloned.1.call-start = ((), (), s32[]{:S(2)}) async-start(), calls=%async_computation.12 | async-start | bytes 5308416 | tf_op jit(solution)/shard_map/all_gather | solution.py:159
  329.1 11.4 copy-start.64
  329.1 11.3 copy-start.63
  329.2 11.4 copy-start.62
  329.2 11.4 copy-start.61
  329.2 11.4 copy-start.60
  335.3 63.3 %copy-start.6 = (bf16[2,512,768]{2,1,0:T(8,128)(2,1)S(1)}, bf16[2,512,768]{2,1,0:T(8,128)(2,1)}, u32[]{:S(2)}) copy-start(bf16[2,512,768]{2,1,0:T(8,128)(2,1)} %param.21) | copy-start | bytes 4718596
  335.3 52.5 %all-to-all-start.2 = ((bf16[2,2048,1,192]{3,0,2,1:T(2,128)(2,1)}), bf16[2,2048,1,192]{3,0,2,1:T(2,128)(2,1)}, u32[]{:S(2)}, u32[]{:S(2)}) async-start(bf16[2,2048,1,192]{3,0,2,1:T(2,128)(2,1)} %bitcast.418), calls=%async_computation.2 | async-start | bytes 4194304 | tf_op jit(solution)/shard_map/all_to_all | solution.py:195
  340.5 747.7 %reduce-scatter.7.cloned.1.call-start = ((), (), s32[]{:S(2)}) async-start(), calls=%async_computation.14 | async-start | bytes 2654208 | tf_op jit(solution)/shard_map/reduce_scatter | solution.py:289
  404.2 11.2 copy-start.15
  415.4 13.7 %copy-start.54 = (s32[2,512]{1,0:T(2,128)S(1)}, s32[2,512]{1,0:T(2,128)}, u32[]{:S(2)}) copy-start(s32[2,512]{1,0:T(2,128)} %param.25) | copy-start | bytes 12292
  415.5 13.7 %copy-start.55 = (s32[2,512]{1,0:T(2,128)S(1)}, s32[2,512]{1,0:T(2,128)}, u32[]{:S(2)}) copy-start(s32[2,512]{1,0:T(2,128)} %param.24) | copy-start | bytes 12292
  470.0 22.1 %slice-start.4 = ((s8[4718592]{0:T(1024)(128)(4,1)}), s8[4194304]{0:T(1024)(128)(4,1)S(1)}, s32[]{:S(2)}) async-start(s8[4718592]{0:T(1024)(128)(4,1)} %bitcast.450), calls=%async_computation.22 | async-start | bytes 8388608
  473.6 18.5 %copy-start.35 = (bf16[1024,768]{1,0:T(8,128)(2,1)}, bf16[1024,768]{1,0:T(8,128)(2,1)S(1)}, u32[]{:S(2)}) copy-start(bf16[1024,768]{1,0:T(8,128)(2,1)S(1)} %get-tuple-element.202) | copy-start | bytes 4718596
  473.6 18.5 %slice-start.5 = ((s8[4718592]{0:T(1024)(128)(4,1)}), s8[524288]{0:T(1024)(128)(4,1)S(1)}, s32[]{:S(2)}) async-start(s8[4718592]{0:T(1024)(128)(4,1)} %bitcast.450), calls=%async_computation.23 | async-start | bytes 1048576
  492.1 6.2 copy-start.25
  507.7 592.7 %reduce-scatter.9.cloned.1.call-start = ((), (), s32[]{:S(2)}) async-start(), calls=%async_computation.15 | async-start | bytes 10616832 | tf_op jit(solution)/shard_map/reduce_scatter | solution.py:293
  524.4 8.4 copy-start.36
  528.6 40.6 %all-to-all-start.3 = ((bf16[2,512,4,192]{1,0,3,2:T(2,128)(2,1)}), bf16[2,512,4,192]{1,0,3,2:T(2,128)(2,1)S(1)}, u32[]{:S(2)}, u32[]{:S(2)}) async-start(bf16[2,512,4,192]{1,0,3,2:T(2,128)(2,1)} %reshape.704), calls=%async_computation.3 | async-start | bytes 3145728 | tf_op jit(solution)/shard_map/all_to_all | solution.py:263
  532.8 569.8 %reduce-scatter.11.cloned.1.call-start = ((), (), s32[]{:S(2)}) async-start(), calls=%async_computation.16 | async-start | bytes 10616832 | tf_op jit(solution)/shard_map/reduce_scatter | solution.py:295
  572.6 27.3 %copy-start.26 = (f32[3,512]{1,0:T(4,128)}, f32[3,512]{1,0:T(4,128)S(1)}, u32[]{:S(2)}) copy-start(f32[3,512]{1,0:T(4,128)S(1)} %get-tuple-element.435) | copy-start | bytes 18436 | tf_op jit(solution)/shard_map/while
  576.0 6.2 copy-start.12
  576.0 18.4 %copy-start.10 = (bf16[512,1,1,192]{0,3,2,1:T(8,128)(2,1)}, bf16[512,1,1,192]{0,3,2,1:T(8,128)(2,1)S(1)}, u32[]{:S(2)}) copy-start(bf16[512,1,1,192]{0,3,2,1:T(8,128)(2,1)S(1)} %get-tuple-element.433) | copy-start | bytes 589828 | tf_op jit(solution)/shard_map/while
  580.3 42.4 %copy-start.4 = (pred[512,2048]{1,0:T(8,128)(4,1)}, pred[512,2048]{1,0:T(8,128)(4,1)S(1)}, u32[]{:S(2)}) copy-start(pred[512,2048]{1,0:T(8,128)(4,1)S(1)} %get-tuple-element.448) | copy-start | bytes 3145732 | tf_op jit(solution)/shard_map/while
  582.2 4.6 copy-start
  659.2 6.5 copy-start.3
  659.2 7.7 slice-start
  671.3 6.6 copy-start.16
  671.3 6.6 copy-start.65
  696.7 18.2 %copy-start.11 = (bf16[512,1,1,192]{0,3,2,1:T(8,128)(2,1)S(1)}, bf16[512,1,1,192]{0,3,2,1:T(8,128)(2,1)}, u32[]{:S(2)}) copy-start(bf16[512,1,1,192]{0,3,2,1:T(8,128)(2,1)} %copy-done.10) | copy-start | bytes 589828 | tf_op jit(solution)/shard_map/while
  714.9 4.6 copy-start.2
  729.0 27.3 %copy-start.26 = (f32[3,512]{1,0:T(4,128)}, f32[3,512]{1,0:T(4,128)S(1)}, u32[]{:S(2)}) copy-start(f32[3,512]{1,0:T(4,128)S(1)} %get-tuple-element.435) | copy-start | bytes 18436 | tf_op jit(solution)/shard_map/while
  732.4 6.2 copy-start.12
  732.4 18.5 %copy-start.10 = (bf16[512,1,1,192]{0,3,2,1:T(8,128)(2,1)}, bf16[512,1,1,192]{0,3,2,1:T(8,128)(2,1)S(1)}, u32[]{:S(2)}) copy-start(bf16[512,1,1,192]{0,3,2,1:T(8,128)(2,1)S(1)} %get-tuple-element.433) | copy-start | bytes 589828 | tf_op jit(solution)/shard_map/while
  736.8 41.9 %copy-start.4 = (pred[512,2048]{1,0:T(8,128)(4,1)}, pred[512,2048]{1,0:T(8,128)(4,1)S(1)}, u32[]{:S(2)}) copy-start(pred[512,2048]{1,0:T(8,128)(4,1)S(1)} %get-tuple-element.448) | copy-start | bytes 3145732 | tf_op jit(solution)/shard_map/while
  738.6 4.6 copy-start
  811.9 5.7 copy-start.3
  811.9 6.9 slice-start
  823.1 6.3 copy-start.16
  823.1 6.3 copy-start.65
  847.8 18.1 %copy-start.11 = (bf16[512,1,1,192]{0,3,2,1:T(8,128)(2,1)S(1)}, bf16[512,1,1,192]{0,3,2,1:T(8,128)(2,1)}, u32[]{:S(2)}) copy-start(bf16[512,1,1,192]{0,3,2,1:T(8,128)(2,1)} %copy-done.10) | copy-start | bytes 589828 | tf_op jit(solution)/shard_map/while
  902.9 5.5 copy-start.7
  902.9 5.5 copy-start.40
  902.9 5.5 copy-start.46
  902.9 5.5 copy-start.48
  902.9 5.5 copy-start.52
  903.0 143.4 %all-to-all-start.4 = ((bf16[2,2048,3,1,192]{4,0,3,2,1:T(2,128)(2,1)}), bf16[2,2048,3,1,192]{4,0,3,2,1:T(2,128)(2,1)}, u32[]{:S(2)}, u32[]{:S(2)}) async-start(bf16[2,2048,3,1,192]{4,0,3,2,1:T(2,128)(2,1)} %copy.95), calls=%async_computation.4 | async-start | bytes 12582912 | tf_op jit(solution)/shard_map/all_to_all | solution.py:271
  908.3 241.0 %reduce-scatter.5.cloned.1.call-start = ((), (), s32[]{:S(2)}) async-start(), calls=%async_computation.13 | async-start | bytes 7962624 | tf_op jit(solution)/shard_map/reduce_scatter | solution.py:287
  1084.7 5.2 copy-start.42
  1084.7 145.5 %all-reduce.22.cloned.1.call-start = ((), (), s32[]{:S(2)}) async-start(), calls=%async_computation.17 | async-start | bytes 3538944 | tf_op jit(solution)/shard_map/psum | solution.py:301
  1104.7 51.4 %copy-start.50 = (f32[1,4,2,128]{3,1,2,0:T(4,128)S(1)}, f32[1,4,2,128]{3,1,2,0:T(4,128)}, u32[]{:S(2)}) copy-start(f32[1,4,2,128]{3,1,2,0:T(4,128)} %copy-done.49) | copy-start | bytes 12292
  1104.7 51.4 %copy-start.44 = (f32[1024]{0:T(1024)S(1)}, f32[1024]{0:T(1024)}, u32[]{:S(2)}) copy-start(f32[1024]{0:T(1024)} %copy-done.43) | copy-start | bytes 12292
  1151.4 7.8 copy-start.51
  1151.4 7.8 copy-start.53
  1151.4 7.8 copy-start.56
  1151.4 7.8 copy-start.58
  1151.4 7.8 copy-start.59
  (52 other events, 124.0 us)
Sparse Core Ops, SparseCore 0:
  9.9 36.8 all-gather.5
  48.7 24.0 all-gather.7
  74.7 38.9 all-gather.9
  201.0 40.8 all-gather.11
  507.8 43.0 reduce-scatter.6
  554.7 76.4 reduce-scatter.8
  635.2 76.4 reduce-scatter.10
  1084.8 64.5 reduce-scatter.4
  1153.2 76.9 all-reduce.21
where the time goes:
time: 1260 us; the launch traced here: 1250 us
  waiting for transfers between devices  373 us (30%)
  matrix products  356 us (28%)
  other arithmetic  177 us (14%)
  local copies, waits for them, and re-layouts  159 us (13%)
  blocking collectives  112 us (9%)
  loops' own time  24.8 us (2%)
  starting transfers between devices  23.5 us (2%)
  between operations  21.1 us (2%)
    all_to_all x1, waiting for transfers between devices, local(): lax.all_to_all(grad_joint_heads, 'seq', split_axis=1, concat_axis=3, tile...  137 us
    all_to_all x1, waiting for transfers between devices, local(): lax.all_to_all(joint_low, 'seq', split_axis=3, concat_axis=1, tiled=True)  102 us
    convert_element_type x4, other arithmetic, back_sequence(): grad_scores = (probs * (grad_probs - center)).astype(jnp.bfloat16)  85.3 us
    dot_general x8, matrix products, back_sequence(): jnp.einsum('qhd,khd->hqk', grad_block, values, preferred_element_type=jnp...  73.9 us
    dot_general x16, matrix products, block_scores(): jnp.einsum('qhd,khd->hqk', query_block, keys, preferred_element_type=jnp....  54.2 us
    unnamed x2, blocking collectives  51.7 us
    dot_general x8, matrix products, back_sequence(): jnp.einsum('hqk,qhd->khd', probs_low, grad_block, preferred_element_type=...  46.4 us
    reduce_scatter x1, waiting for transfers between devices, local(): lax.psum_scatter(grad_jointweight, 'fsdp', scatter_dimension=0, tiled=True)  44.6 us
  transfers between devices with their start and end apart: 14, of which 6 were waited for; matrix products, arithmetic and copies ran while one was open for 48% of the time, Pallas kernels for 0%

commit v1 on v0

--- a/solution.py
+++ b/solution.py
@@ -213,7 +213,8 @@
     layer_out = result.astype(jnp.bfloat16).reshape(tokens.shape)
     error = result - teacher.astype(jnp.float32).reshape(rows, width)
     local_sum = jnp.sum(weight * jnp.sum(error * error, -1))
-    total_sum, total_count = lax.psum((local_sum, local_count), ("fsdp", "seq"))
+    hold_the_stops_all = lambda a0: lax.psum(lax.psum(a0, axis_name="seq"), axis_name="fsdp")
+    total_sum, total_count = hold_the_stops_all((local_sum, local_count))
     distill_loss = total_sum / (width * total_count)
     token_total = rows * lax.axis_size("fsdp") * groups
     factor = token_total / total_count

time: 1260 us -> 1240 us (0.984)
  blocking collectives: 112 us -> 96.2 us
    unnamed x2 -> x1, blocking collectives: 51.7 us -> 26.6 us
    psum x1 -> x3, blocking collectives: 39.5 us -> 48.9 us  [the longest x2 38.5 us: local(): lax.psum(lax.psum(a0, axis_name='seq'), axis_name='fsdp')]
  transfers between devices with their start and end apart: 14 -> 14, of which waited for: 6 -> 6; matrix products, arithmetic and copies ran while one was open for 48% -> 49% of each run, Pallas kernels for 0% -> 0%
where the time goes in v1:
time: 1240 us; the launch traced here: 1230 us
  waiting for transfers between devices  372 us (30%)
  matrix products  355 us (29%)
  other arithmetic  179 us (14%)
  local copies, waits for them, and re-layouts  159 us (13%)
  blocking collectives  96.2 us (8%)
  loops' own time  24.8 us (2%)
  starting transfers between devices  22.9 us (2%)
  between operations  21.2 us (2%)
    all_to_all x1, waiting for transfers between devices, local(): lax.all_to_all(grad_joint_heads, 'seq', split_axis=1, concat_axis=3, tile...  137 us
    all_to_all x1, waiting for transfers between devices, local(): lax.all_to_all(joint_low, 'seq', split_axis=3, concat_axis=1, tiled=True)  102 us
    convert_element_type x4, other arithmetic, back_sequence(): grad_scores = (probs * (grad_probs - center)).astype(jnp.bfloat16)  86.1 us
    dot_general x8, matrix products, back_sequence(): jnp.einsum('qhd,khd->hqk', grad_block, values, preferred_element_type=jnp...  73.7 us
    dot_general x16, matrix products, block_scores(): jnp.einsum('qhd,khd->hqk', query_block, keys, preferred_element_type=jnp....  54.3 us
    dot_general x8, matrix products, back_sequence(): jnp.einsum('hqk,qhd->khd', probs_low, grad_block, preferred_element_type=...  46 us
    reduce_scatter x1, waiting for transfers between devices, local(): lax.psum_scatter(grad_jointweight, 'fsdp', scatter_dimension=0, tiled=True)  43.2 us
    psum x2, blocking collectives, local(): lax.psum(lax.psum(a0, axis_name='seq'), axis_name='fsdp')  38.5 us
  transfers between devices with their start and end apart: 14, of which 6 were waited for; matrix products, arithmetic and copies ran while one was open for 49% of the time, Pallas kernels for 0%

profile of v1, /device:TPU:0, one launch (start us, length us, event | category | flops | bytes accessed | tf_op | source)
XLA Modules:
  0.0 1229.8 jit_solution(10245570874759908243)
XLA Ops:
  19.6 26.6 %all-reduce.17 = (bf16[768]{0:T(1024)(128)(2,1)S(1)}, bf16[768]{0:T(1024)(128)(2,1)S(1)}, bf16[1536]{0:T(1024)(128)(2,1)S(1)}, bf16[768]{0:T(1024)(128)(2,1)}, b...) all-reduce(bf16[768]{0:T(1024)(128)(2,1)S(1)} %dynamic-update-slice, ...), channel_id=1, replica_groups=mesh['fsdp'=8,'seq'=4] {'fsdp'}, use_global_device_ids=true, to_apply=%add.1 | all-reduce | flops 6144 | bytes 24576
  50.1 7.5 add_convert_fusion
  57.6 12.8 %reshape.747 = bf16[2,512,3,4,192]{4,3,2,1,0:T(4,128)(2,1)} reshape(bf16[1024,2304]{1,0:T(8,128)(2,1)} %add_convert_fusion) | data formatting | bytes 9437184 | tf_op jit(solution)/shard_map/reshape | solution.py:181
  70.5 17.3 %copy.86 = bf16[2,512,3,4,192]{1,0,4,2,3:T(2,128)(2,1)} copy(bf16[2,512,3,4,192]{4,3,2,1,0:T(4,128)(2,1)} %reshape.747) | data formatting | bytes 9437184 | tf_op jit(solution)/shard_map/reshape | solution.py:181
  87.8 5.1 all-to-all-start
  92.9 101.8 %all-to-all-done = bf16[2,512,3,4,192]{1,0,4,2,3:T(2,128)(2,1)} async-done(((bf16[2,512,3,4,192]{1,0,4,2,3:T(2,128)(2,1)}), bf16[2,512,3,4,192]{1,0,4,2,3:T(2,128)(2,1)}, u32[]{:S(2)}, u32[]{:S(2)}) %all-to-all-start) | async-done | bytes 4718624 | tf_op jit(solution)/shard_map/all_to_all | solution.py:190
  199.1 8.1 copy.87
  207.3 8.8 all_to_all.62
  216.1 113.0 %while.22 = (s32[]{:T(128)}, bf16[2,2048,192]{1,2,0:T(8,128)(2,1)}, f32[2,3,2048]{2,1,0:T(4,128)S(1)}, bf16[2,2048,3,1,192]{1,4,2,3,0:T(8,128)(2,1)}, bf16[2,204...) while((s32[]{:T(128)}, bf16[2,2048,192]{1,2,0:T(8,128)(2,1)}, ...), condition=%wide.region_11.12_spmd, body=%wide.region_2.11_spmd.sunk | while | flops 3393599488 | bytes 199532768 | solution.py:79
  243.2 6.9 fusion.302
  263.7 6.9 fusion.307
  291.9 6.9 fusion.302
  312.3 6.9 fusion.307
  329.2 6.1 copy.89
  335.3 5.2 all-to-all-start.2
  340.5 8.9 all-gather
  349.4 38.3 %all-to-all-done.2 = bf16[2,2048,1,192]{3,0,2,1:T(2,128)(2,1)} async-done(((bf16[2,2048,1,192]{3,0,2,1:T(2,128)(2,1)}), bf16[2,2048,1,192]{3,0,2,1:T(2,128)(2,1)}, u32[]{:S(2)}, u32[]{:S(2)}) %all-to-all-start.2) | async-done | bytes 1572896 | tf_op jit(solution)/shard_map/all_to_all | solution.py:195
  387.7 9.3 copy.90
  404.2 11.2 fusion.113
  415.4 13.7 %multiply_reduce_fusion.6 = (f32[1024]{0:T(1024)S(1)}, f32[1024,768]{1,0:T(8,128)}) fusion(bf16[2,512,768]{2,1,0:T(8,128)(2,1)} %param.22, f32[768]{0:T(1024)S(1)} %convert_element_type.248, f32[1024,768]{1,0:T(8,128)S(1)} %copy-done.15, bf16[3072,768]{1,0:T(8,128)(2,1)} %all-gather.12.cloned.1.call-done, f32[1024,3072]{1,0:T(8,128)} %fusion.113, ...), kind=kOutput, calls=%fused_computation.184 | convolution fusion | flops 4868013056 | bytes 25185280 | tf_op jit(solution)/shard_map/dot_general | solution.py:211
  429.7 10.4 all-reduce.16
  440.2 13.2 %psum.115 = f32[]{:T(128)} all-reduce(f32[]{:T(128)} %get-tuple-element.182), channel_id=1, replica_groups=mesh['fsdp'=8,'seq'=4] {'fsdp'}, use_global_device_ids=true, to_apply=%region_20.21 | all-reduce | flops 1 | bytes 8 | tf_op jit(solution)/shard_map/psum | solution.py:216
  454.1 5.8 convert_reduce_fusion.3
  459.9 18.4 %convert_reduce_fusion = (f32[3072]{0:T(1024)}, bf16[1024,3072]{1,0:T(8,128)(2,1)S(1)}) fusion(f32[1024,3072]{1,0:T(8,128)} %fusion.113, f32[3072]{0:T(1024)S(1)} %bitcast.448, bf16[1024,768]{1,0:T(8,128)(2,1)S(1)} %get-tuple-element.203, bf16[3072,768]{1,0:T(8,128)(2,1)} %all-gather.12.cloned.1.call-done), kind=kOutput, calls=%fused_computation.151 | convolution fusion | flops 4916769792 | bytes 25190400 | tf_op jit(solution)/shard_map/rd,fd->rf/dot_general | solution.py:245
  478.4 6.1 multiply_reduce_fusion.4
  492.8 11.0 fusion.112
  517.4 13.0 %fusion.114 = f32[3072,768]{1,0:T(8,128)} fusion(bf16[1024,768]{1,0:T(8,128)(2,1)S(1)} %copy-done.36, f32[1024,3072]{1,0:T(8,128)} %fusion.113, f32[3072]{0:T(1024)S(1)} %bitcast.449), kind=kOutput, calls=%fused_computation.222 | convolution fusion | flops 4863295488 | bytes 23605248 | tf_op jit(solution)/shard_map/rf,rd->fd/dot_general | solution.py:242
  530.4 24.6 %all-to-all-done.3 = bf16[2,512,4,192]{1,0,3,2:T(2,128)(2,1)S(1)} async-done(((bf16[2,512,4,192]{1,0,3,2:T(2,128)(2,1)}), bf16[2,512,4,192]{1,0,3,2:T(2,128)(2,1)S(1)}, u32[]{:S(2)}, u32[]{:S(2)}) %all-to-all-start.3) | async-done | bytes 1572896 | tf_op jit(solution)/shard_map/all_to_all | solution.py:264
  557.4 314.9 %while.23 = (s32[]{:T(128)}, bf16[2,2048,3,1,192]{1,4,3,2,0:T(8,128)(2,1)}, bf16[2,2048,3,1,192]{1,4,2,3,0:T(8,128)(2,1)}, bf16[2,2048]{1,0:T(2,128)(2,1)S(1)}, ...) while((s32[]{:T(128)}, ...), condition=%wide.region_28.29_spmd, body=%wide.region_23.28_spmd.sunk | while | flops 8274178048 | bytes 657154752 | solution.py:271
  572.8 7.6 multiply_reduce_fusion.13
  585.9 8.1 multiply_reduce_fusion.16
  594.1 6.6 fusion.360
  600.7 7.9 fusion.361
  608.6 10.3 multiply_reduce_fusion.14
  618.9 26.9 %multiply_convert_fusion.8 = (bf16[3,512,2048]{2,1,0:T(8,128)(2,1)}, bf16[3,512,2048]{2,1,0:T(8,128)(2,1)}) fusion(f32[3,512,2048]{2,1,0:T(8,128)} %get-tuple-element.455, f32[3,512,2048]{2,1,0:T(8,128)} %copy-done, f32[3,512]{1,0:T(4,128)S(1)} %get-tuple-element.456, f32[3,512]{1,0:T(4,128)S(1)} %get-tuple-element.444, ...), kind=kLoop, calls=%fused_computation.68.clone.1 | loop fusion | flops 37748736 | bytes 65036288 | tf_op jit(solution)/shard_map/while/body/eval_jaxpr/convert_element_type | solution.py:106
  645.8 5.7 fusion.369
  657.2 6.3 fusion.362
  663.5 8.0 fusion.363
  671.5 10.7 multiply_reduce_fusion.15
  682.2 18.3 %multiply_convert_fusion.9 = (bf16[3,512,2048]{2,1,0:T(8,128)(2,1)}, bf16[3,512,2048]{2,1,0:T(8,128)(2,1)}) fusion(f32[3,512,2048]{2,1,0:T(8,128)} %get-tuple-element.461, f32[3,512,2048]{2,1,0:T(8,128)} %fusion.362, f32[3,512]{1,0:T(4,128)} %get-tuple-element.462, f32[3,512]{1,0:T(4,128)S(1)} %get-tuple-element.452, ...), kind=kLoop, calls=%fused_computation.62.clone.1 | loop fusion | flops 37748736 | bytes 65036288 | tf_op jit(solution)/shard_map/while/body/eval_jaxpr/convert_element_type | solution.py:106
  728.8 7.6 multiply_reduce_fusion.13
  742.0 8.1 multiply_reduce_fusion.16
  750.1 6.3 fusion.360
  756.4 7.8 fusion.361
  764.2 10.4 multiply_reduce_fusion.14
  774.6 22.8 %multiply_convert_fusion.8 = (bf16[3,512,2048]{2,1,0:T(8,128)(2,1)}, bf16[3,512,2048]{2,1,0:T(8,128)(2,1)}) fusion(f32[3,512,2048]{2,1,0:T(8,128)} %get-tuple-element.455, f32[3,512,2048]{2,1,0:T(8,128)} %copy-done, f32[3,512]{1,0:T(4,128)S(1)} %get-tuple-element.456, f32[3,512]{1,0:T(4,128)S(1)} %get-tuple-element.444, ...), kind=kLoop, calls=%fused_computation.68.clone.1 | loop fusion | flops 37748736 | bytes 65036288 | tf_op jit(solution)/shard_map/while/body/eval_jaxpr/convert_element_type | solution.py:106
  797.5 5.7 fusion.369
  808.7 6.3 fusion.362
  815.0 7.7 fusion.363
  822.7 10.7 multiply_reduce_fusion.15
  833.4 18.0 %multiply_convert_fusion.9 = (bf16[3,512,2048]{2,1,0:T(8,128)(2,1)}, bf16[3,512,2048]{2,1,0:T(8,128)(2,1)}) fusion(f32[3,512,2048]{2,1,0:T(8,128)} %get-tuple-element.461, f32[3,512,2048]{2,1,0:T(8,128)} %fusion.362, f32[3,512]{1,0:T(4,128)} %get-tuple-element.462, f32[3,512]{1,0:T(4,128)S(1)} %get-tuple-element.452, ...), kind=kLoop, calls=%fused_computation.62.clone.1 | loop fusion | flops 37748736 | bytes 65036288 | tf_op jit(solution)/shard_map/while/body/eval_jaxpr/convert_element_type | solution.py:106
  872.3 16.1 %copy.95 = bf16[2,2048,3,1,192]{4,0,3,2,1:T(2,128)(2,1)} copy(bf16[2,2048,3,1,192]{1,4,3,2,0:T(8,128)(2,1)} %get-tuple-element.77) | data formatting | bytes 9437184 | tf_op jit(solution)/shard_map/while | solution.py:271
  888.5 5.4 all-to-all-start.4
  894.6 137.4 %all-to-all-done.4 = bf16[2,2048,3,1,192]{4,0,3,2,1:T(2,128)(2,1)} async-done(((bf16[2,2048,3,1,192]{4,0,3,2,1:T(2,128)(2,1)}), bf16[2,2048,3,1,192]{4,0,3,2,1:T(2,128)(2,1)}, u32[]{:S(2)}, u32[]{:S(2)}) %all-to-all-start.4) | async-done | bytes 4718624 | tf_op jit(solution)/shard_map/all_to_all | solution.py:272
  1032.0 17.0 %copy.102 = bf16[2,4,512,3,1,192]{2,1,5,3,0,4:T(4,128)(2,1)} copy(bf16[2,4,512,3,1,192]{5,0,3,2,1,4:T(2,128)(2,1)} %bitcast.59) | data formatting | bytes 9437184 | tf_op jit(solution)/shard_map/all_to_all | solution.py:272
  1049.0 9.3 copy.97
  1064.3 6.0 fusion.133
  1074.9 10.8 fusion.117
  1090.0 43.2 %reduce-scatter.5.cloned.1.call-done = f32[96,2304]{1,0:T(8,128)} async-done(((f32[768,2304]{1,0:T(8,128)}), f32[96,2304]{1,0:T(8,128)}) %reduce-scatter.5.cloned.1.call-update) | async-done | bytes 884752 | tf_op jit(solution)/shard_map/reduce_scatter | solution.py:288
  1135.3 4.3 convert_reduce_fusion.1
  1143.0 25.2 %all-reduce.15 = (f32[]{:T(128)}, bf16[768]{0:T(1024)(128)(2,1)S(1)}, bf16[768]{0:T(1024)(128)(2,1)S(1)}, bf16[1536]{0:T(1024)(128)(2,1)S(1)}, bf16[768]{0:T(102...) all-reduce(f32[]{:T(128)} %get-tuple-element.181, ...), channel_id=1, replica_groups=mesh['fsdp'=8,'seq'=4] {'fsdp'}, use_global_device_ids=true, to_apply=%region_17.18 | all-reduce | flops 9217 | bytes 55304 | tf_op jit(solution)/shard_map/psum | solution.py:216
  1168.8 11.8 all-reduce.18
  1185.5 4.3 add_convert_fusion.1
  1189.9 24.1 %all-reduce.22.cloned.1.call-done = (bf16[96,2304]{1,0:T(8,128)(2,1)}, bf16[96,768]{1,0:T(8,128)(2,1)}, bf16[96,3072]{1,0:T(8,128)(2,1)}, bf16[384,768]{1,0:T(8,128)(2,1)}) async-done(((bf16[96,2304]{1,0:T(8,128)(2,1)}, bf16[96,768]{1,0:T(8,128)(2,1)}, bf16[96,3072]{1,0:T(8,128)(2,1)}, bf16[384,768]{1,0:T(8,128)(2,1)}), (bf16[96,2304]{1,0:T(8,128)(2,1)}, bf16[96,768]{1,0:T(8,128)(2,1)}, ...) | async-done | bytes 1769488 | tf_op jit(solution)/shard_map/psum | solution.py:302
  (430 shorter events, 229.7 us)
Async XLA Ops:
  7.2 42.3 %copy-start.5 = (bf16[2,512,768]{2,1,0:T(8,128)(2,1)S(1)}, bf16[2,512,768]{2,1,0:T(8,128)(2,1)}, u32[]{:S(2)}) copy-start(bf16[2,512,768]{2,1,0:T(8,128)(2,1)} %param.21) | copy-start | bytes 4718596
  7.2 42.9 %all-gather.6.cloned.1.call-start = ((), (), s32[]{:S(2)}) async-start(), calls=%async_computation.9 | async-start | bytes 3981312 | tf_op jit(solution)/shard_map/all_gather | solution.py:151
  7.9 390.6 %all-gather.8.cloned.1.call-start = ((), (), s32[]{:S(2)}) async-start(), calls=%async_computation.10 | async-start | bytes 1327104 | tf_op jit(solution)/shard_map/all_gather | solution.py:153
  8.7 395.5 %all-gather.10.cloned.1.call-start = ((), (), s32[]{:S(2)}) async-start(), calls=%async_computation.11 | async-start | bytes 5308416 | tf_op jit(solution)/shard_map/all_gather | solution.py:157
  87.8 5.1 copy-start.59
  87.8 106.9 %all-to-all-start = ((bf16[2,512,3,4,192]{1,0,4,2,3:T(2,128)(2,1)}), bf16[2,512,3,4,192]{1,0,4,2,3:T(2,128)(2,1)}, u32[]{:S(2)}, u32[]{:S(2)}) async-start(bf16[2,512,3,4,192]{1,0,4,2,3:T(2,128)(2,1)} %copy.86), calls=%async_computation | async-start | bytes 9437184 | tf_op jit(solution)/shard_map/all_to_all | solution.py:190
  195.3 20.8 %all-to-all-start.1 = ((bf16[2,512,1,4,1]{1,0,4,2,3:T(2,128)(2,1)}), bf16[2,512,1,4,1]{1,0,4,2,3:T(2,128)(2,1)S(1)}, u32[]{:S(2)}, u32[]{:S(2)}) async-start(bf16[2,512,1,4,1]{1,0,4,2,3:T(2,128)(2,1)} %broadcast_in_dim.114), calls=%async_computation.1 | async-start | bytes 16384 | tf_op jit(solution)/shard_map/all_to_all | solution.py:191
  198.5 216.8 %all-gather.12.cloned.1.call-start = ((), (), s32[]{:S(2)}) async-start(), calls=%async_computation.12 | async-start | bytes 5308416 | tf_op jit(solution)/shard_map/all_gather | solution.py:159
  329.1 11.3 copy-start.64
  329.1 11.3 copy-start.63
  329.1 11.3 copy-start.62
  329.1 11.3 copy-start.61
  329.2 11.3 copy-start.60
  335.3 63.3 %copy-start.6 = (bf16[2,512,768]{2,1,0:T(8,128)(2,1)S(1)}, bf16[2,512,768]{2,1,0:T(8,128)(2,1)}, u32[]{:S(2)}) copy-start(bf16[2,512,768]{2,1,0:T(8,128)(2,1)} %param.21) | copy-start | bytes 4718596
  335.3 52.5 %all-to-all-start.2 = ((bf16[2,2048,1,192]{3,0,2,1:T(2,128)(2,1)}), bf16[2,2048,1,192]{3,0,2,1:T(2,128)(2,1)}, u32[]{:S(2)}, u32[]{:S(2)}) async-start(bf16[2,2048,1,192]{3,0,2,1:T(2,128)(2,1)} %bitcast.418), calls=%async_computation.2 | async-start | bytes 4194304 | tf_op jit(solution)/shard_map/all_to_all | solution.py:195
  340.4 732.8 %reduce-scatter.7.cloned.1.call-start = ((), (), s32[]{:S(2)}) async-start(), calls=%async_computation.14 | async-start | bytes 2654208 | tf_op jit(solution)/shard_map/reduce_scatter | solution.py:290
  404.1 11.2 copy-start.15
  415.4 13.7 %copy-start.54 = (s32[2,512]{1,0:T(2,128)S(1)}, s32[2,512]{1,0:T(2,128)}, u32[]{:S(2)}) copy-start(s32[2,512]{1,0:T(2,128)} %param.25) | copy-start | bytes 12292
  415.4 13.7 %copy-start.55 = (s32[2,512]{1,0:T(2,128)S(1)}, s32[2,512]{1,0:T(2,128)}, u32[]{:S(2)}) copy-start(s32[2,512]{1,0:T(2,128)} %param.24) | copy-start | bytes 12292
  454.1 24.2 %slice-start.4 = ((s8[4718592]{0:T(1024)(128)(4,1)}), s8[4194304]{0:T(1024)(128)(4,1)S(1)}, s32[]{:S(2)}) async-start(s8[4718592]{0:T(1024)(128)(4,1)} %bitcast.450), calls=%async_computation.22 | async-start | bytes 8388608
  459.9 18.5 %copy-start.35 = (bf16[1024,768]{1,0:T(8,128)(2,1)}, bf16[1024,768]{1,0:T(8,128)(2,1)S(1)}, u32[]{:S(2)}) copy-start(bf16[1024,768]{1,0:T(8,128)(2,1)S(1)} %get-tuple-element.203) | copy-start | bytes 4718596
  459.9 18.5 %slice-start.5 = ((s8[4718592]{0:T(1024)(128)(4,1)}), s8[524288]{0:T(1024)(128)(4,1)S(1)}, s32[]{:S(2)}) async-start(s8[4718592]{0:T(1024)(128)(4,1)} %bitcast.450), calls=%async_computation.23 | async-start | bytes 1048576
  478.4 6.1 copy-start.25
  492.7 593.0 %reduce-scatter.9.cloned.1.call-start = ((), (), s32[]{:S(2)}) async-start(), calls=%async_computation.15 | async-start | bytes 10616832 | tf_op jit(solution)/shard_map/reduce_scatter | solution.py:294
  509.5 7.8 copy-start.36
  513.7 41.3 %all-to-all-start.3 = ((bf16[2,512,4,192]{1,0,3,2:T(2,128)(2,1)}), bf16[2,512,4,192]{1,0,3,2:T(2,128)(2,1)S(1)}, u32[]{:S(2)}, u32[]{:S(2)}) async-start(bf16[2,512,4,192]{1,0,3,2:T(2,128)(2,1)} %reshape.704), calls=%async_computation.3 | async-start | bytes 3145728 | tf_op jit(solution)/shard_map/all_to_all | solution.py:264
  517.3 570.6 %reduce-scatter.11.cloned.1.call-start = ((), (), s32[]{:S(2)}) async-start(), calls=%async_computation.16 | async-start | bytes 10616832 | tf_op jit(solution)/shard_map/reduce_scatter | solution.py:296
  558.5 27.5 %copy-start.26 = (f32[3,512]{1,0:T(4,128)}, f32[3,512]{1,0:T(4,128)S(1)}, u32[]{:S(2)}) copy-start(f32[3,512]{1,0:T(4,128)S(1)} %get-tuple-element.436) | copy-start | bytes 18436 | tf_op jit(solution)/shard_map/while
  561.8 6.2 copy-start.12
  561.8 18.6 %copy-start.10 = (bf16[512,1,1,192]{0,3,2,1:T(8,128)(2,1)}, bf16[512,1,1,192]{0,3,2,1:T(8,128)(2,1)S(1)}, u32[]{:S(2)}) copy-start(bf16[512,1,1,192]{0,3,2,1:T(8,128)(2,1)S(1)} %get-tuple-element.434) | copy-start | bytes 589828 | tf_op jit(solution)/shard_map/while
  566.2 42.4 %copy-start.4 = (pred[512,2048]{1,0:T(8,128)(4,1)}, pred[512,2048]{1,0:T(8,128)(4,1)S(1)}, u32[]{:S(2)}) copy-start(pred[512,2048]{1,0:T(8,128)(4,1)S(1)} %get-tuple-element.449) | copy-start | bytes 3145732 | tf_op jit(solution)/shard_map/while
  568.0 4.8 copy-start
  645.8 5.7 copy-start.3
  645.8 6.9 slice-start
  657.2 6.3 copy-start.16
  657.2 6.3 copy-start.65
  682.2 18.3 %copy-start.11 = (bf16[512,1,1,192]{0,3,2,1:T(8,128)(2,1)S(1)}, bf16[512,1,1,192]{0,3,2,1:T(8,128)(2,1)}, u32[]{:S(2)}) copy-start(bf16[512,1,1,192]{0,3,2,1:T(8,128)(2,1)} %copy-done.10) | copy-start | bytes 589828 | tf_op jit(solution)/shard_map/while
  700.6 4.6 copy-start.2
  714.7 27.3 %copy-start.26 = (f32[3,512]{1,0:T(4,128)}, f32[3,512]{1,0:T(4,128)S(1)}, u32[]{:S(2)}) copy-start(f32[3,512]{1,0:T(4,128)S(1)} %get-tuple-element.436) | copy-start | bytes 18436 | tf_op jit(solution)/shard_map/while
  718.0 6.2 copy-start.12
  718.0 18.5 %copy-start.10 = (bf16[512,1,1,192]{0,3,2,1:T(8,128)(2,1)}, bf16[512,1,1,192]{0,3,2,1:T(8,128)(2,1)S(1)}, u32[]{:S(2)}) copy-start(bf16[512,1,1,192]{0,3,2,1:T(8,128)(2,1)S(1)} %get-tuple-element.434) | copy-start | bytes 589828 | tf_op jit(solution)/shard_map/while
  722.4 41.9 %copy-start.4 = (pred[512,2048]{1,0:T(8,128)(4,1)}, pred[512,2048]{1,0:T(8,128)(4,1)S(1)}, u32[]{:S(2)}) copy-start(pred[512,2048]{1,0:T(8,128)(4,1)S(1)} %get-tuple-element.449) | copy-start | bytes 3145732 | tf_op jit(solution)/shard_map/while
  724.2 4.6 copy-start
  797.5 5.7 copy-start.3
  797.5 6.9 slice-start
  808.7 6.3 copy-start.16
  808.7 6.3 copy-start.65
  833.4 18.0 %copy-start.11 = (bf16[512,1,1,192]{0,3,2,1:T(8,128)(2,1)S(1)}, bf16[512,1,1,192]{0,3,2,1:T(8,128)(2,1)}, u32[]{:S(2)}) copy-start(bf16[512,1,1,192]{0,3,2,1:T(8,128)(2,1)} %copy-done.10) | copy-start | bytes 589828 | tf_op jit(solution)/shard_map/while
  851.4 4.6 copy-start.2
  888.5 5.5 copy-start.7
  888.5 5.5 copy-start.40
  888.5 5.5 copy-start.46
  888.5 5.5 copy-start.48
  888.5 5.5 copy-start.51
  888.5 143.5 %all-to-all-start.4 = ((bf16[2,2048,3,1,192]{4,0,3,2,1:T(2,128)(2,1)}), bf16[2,2048,3,1,192]{4,0,3,2,1:T(2,128)(2,1)}, u32[]{:S(2)}, u32[]{:S(2)}) async-start(bf16[2,2048,3,1,192]{4,0,3,2,1:T(2,128)(2,1)} %copy.95), calls=%async_computation.4 | async-start | bytes 12582912 | tf_op jit(solution)/shard_map/all_to_all | solution.py:272
  893.9 239.4 %reduce-scatter.5.cloned.1.call-start = ((), (), s32[]{:S(2)}) async-start(), calls=%async_computation.13 | async-start | bytes 7962624 | tf_op jit(solution)/shard_map/reduce_scatter | solution.py:288
  1070.3 143.7 %all-reduce.22.cloned.1.call-start = ((), (), s32[]{:S(2)}) async-start(), calls=%async_computation.17 | async-start | bytes 3538944 | tf_op jit(solution)/shard_map/psum | solution.py:302
  1090.0 49.9 %copy-start.50 = (f32[1,4,2,128]{3,1,2,0:T(4,128)S(1)}, f32[1,4,2,128]{3,1,2,0:T(4,128)}, u32[]{:S(2)}) copy-start(f32[1,4,2,128]{3,1,2,0:T(4,128)} %copy-done.49) | copy-start | bytes 12292
  1090.0 50.0 %copy-start.44 = (f32[1024]{0:T(1024)S(1)}, f32[1024]{0:T(1024)}, u32[]{:S(2)}) copy-start(f32[1024]{0:T(1024)} %copy-done.43) | copy-start | bytes 12292
  1135.2 7.8 copy-start.52
  1135.2 7.8 copy-start.53
  1135.2 7.8 copy-start.56
  1135.2 7.8 copy-start.57
  1135.3 7.8 copy-start.58
  (52 other events, 122.8 us)
Sparse Core Ops, SparseCore 0:
  9.9 36.8 all-gather.5
  48.7 24.0 all-gather.7
  74.7 38.9 all-gather.9
  200.9 40.8 all-gather.11
  492.8 39.7 reduce-scatter.6
  536.4 76.4 reduce-scatter.8
  616.8 76.4 reduce-scatter.10
  1070.5 62.7 reduce-scatter.4
  1137.0 76.9 all-reduce.21
